TPU v7x, 32 devices: a whole 2x2x4 slice. The times are simulated.
32 devices in a mesh: dp: 4 (over y, x), head: 8 (over z, core).
Axes of the slice: x: 2, y: 2, z: 4, core: 2. Of those that a mesh axis runs over, the one named last changes fastest.
Arguments:
- latents: bfloat16 [512, 512], P('dp'), may hold values from -6 to 6
- targets: bfloat16 [512, 32768], P('dp', 'head'), may hold values from -6 to 6
- kv_weight: bfloat16 [512, 32768], P(None, 'head'), may hold values from -0.25 to 0.25
- momentum: float32 [512, 8, 4096], P(None, 'head', 'dp'), may hold values from -120 to 120
Outputs:
- momentum_out: float32 [512, 8, 4096], P(None, 'head', 'dp')
- update: float32 [512, 8, 4096], P(None, 'head', 'dp')
All inputs are finite; a program needn't handle non-finite values.
Results may differ from a plain program's by a relative error of at most 0.0003.
The roundings to bfloat16 on the way count: a program that leaves them out, or rounds other values in their place, can miss the bound.
Values may be sent and summed in bfloat16 or wider, within the bound.
No kernel may reach another device: no remote copies, remote signals or barrier semaphores. Data moves between devices by JAX's collectives and lax.ppermute only.
A program may use at most 64 MiB of HBM per device.

v0:
```python
import math
import jax
import jax.numpy as jnp
from jax import lax
from jax.sharding import PartitionSpec as P

C = 32768
ITERS = 2
decay_rate = 0.95
linear_coef = 3.4445
square_coef = -4.775
quint_coef = 2.0315
epsilon = 1e-07


def gram_total(iterate):
    local_gram = lax.dot_general(
        iterate, iterate, (((1,), (1,)), ((), ())), precision=lax.Precision.HIGHEST
    )
    return lax.psum(local_gram, ("dp", "head"))


def local(latents, targets, kv_weight, momentum):
    latent_width = momentum.shape[0]
    sub_width = momentum.shape[2]
    total_tokens = latents.shape[0] * lax.axis_size("dp")
    residual = (
        jnp.dot(latents, kv_weight, preferred_element_type=jnp.float32)
        - targets.astype(jnp.float32)
    ).astype(jnp.bfloat16)
    columns = lax.all_to_all(residual, "dp", split_axis=1, concat_axis=0, tiled=True)
    gathered = lax.all_gather(latents, "dp", axis=0, tiled=True)
    gradient = lax.dot_general(
        gathered, columns, (((0,), (0,)), ((), ())), preferred_element_type=jnp.float32
    )
    gradient = gradient * (1.0 / math.sqrt(total_tokens))
    previous = momentum.reshape(latent_width, sub_width)
    momentum_new = decay_rate * previous + gradient
    nesterov = gradient + decay_rate * momentum_new
    squares = lax.psum(jnp.sum(nesterov * nesterov), ("dp", "head"))
    inverse = 1.0 / (jnp.sqrt(squares) + epsilon)
    iterate = nesterov * inverse
    gram_matrix = gram_total(iterate)
    for iteration in range(ITERS):
        if iteration > 0:
            gram_matrix = gram_total(iterate)
        polynomial = square_coef * gram_matrix + quint_coef * jnp.dot(
            gram_matrix, gram_matrix, precision=lax.Precision.HIGHEST
        )
        iterate = linear_coef * iterate + jnp.dot(
            polynomial, iterate, precision=lax.Precision.HIGHEST
        )
    update = iterate * math.sqrt(C)
    return (
        momentum_new.reshape(latent_width, 1, sub_width),
        update.reshape(latent_width, 1, sub_width),
    )


def solution(mesh):
    return jax.shard_map(
        local,
        mesh=mesh,
        in_specs=(P("dp", None), P("dp", "head"), P(None, "head"), P(None, "head", "dp")),
        out_specs=(P(None, "head", "dp"), P(None, "head", "dp")),
        check_vma=False,
    )
```

profile of v0, /device:TPU:0, one launch (start us, length us, event | category | flops | bytes accessed | tf_op | source)
XLA Modules:
  0.0 388.6 jit_solution(8422459653737256256)
XLA Ops:
  7.2 3.2 fusion
  10.4 0.0 copy-start.2
  10.4 1.0 copy.21
  11.5 5.2 %all-to-all-start = ((bf16[128,4,1024]{2,0,1:T(8,128)(2,1)}), bf16[128,4,1024]{2,0,1:T(8,128)(2,1)S(1)}, u32[]{:S(2)}, u32[]{:S(2)}) async-start(bf16[128,4,1024]{2,0,1:T(8,128)(2,1)} %bitcast.58), calls=%async_computation | async-start | bytes 2097152 | tf_op jit(solution)/shard_map/all_to_all | solution.py:31
  16.7 4.4 %copy.11 = f32[512,1,1024]{0,2,1:T(8,128)} copy(f32[512,1,1024]{2,1,0:T(1,128)S(1)} %copy-done.2) | data formatting | bytes 4194304 | tf_op args[3]
  21.1 15.9 %all_gather.3 = bf16[512,512]{1,0:T(8,128)(2,1)} all-gather(bf16[128,512]{1,0:T(8,128)(2,1)S(1)} %copy-done.3), channel_id=1, replica_groups=mesh['dp'=4,'head'=8] {'dp'}, dimensions={0}, use_global_device_ids=true | all-gather | bytes 655360 | tf_op jit(solution)/shard_map/all_gather | solution.py:32
  37.0 0.0 all-to-all-done
  37.0 1.9 fusion.12
  38.9 0.0 copy-start
  38.9 2.6 multiply_reduce_fusion
  41.5 39.8 %psum.21 = f32[]{:T(128)} all-reduce(f32[]{:T(128)} %get-tuple-element.6), channel_id=1, replica_groups=mesh['dp'=4,'head'=8] {'dp','head'}, use_global_device_ids=true, to_apply=%region_1.0 | all-reduce | flops 1 | bytes 8 | tf_op jit(solution)/shard_map/psum | solution.py:40
  82.0 7.5 %fusion.3 = f32[512,512]{1,0:T(8,128)} fusion(f32[]{:T(128)S(6)} %div.3, f32[1024,512]{1,0:T(8,128)S(1)} %fusion.12, f32[512,1,1024]{0,2,1:T(8,128)} %copy.11), kind=kOutput, calls=%fused_computation.9 | convolution fusion | flops 3224371200 | bytes 5242884 | tf_op jit(solution)/shard_map/dot_general | solution.py:17
  89.4 0.0 all-reduce.3.cloned.1.call-update
  89.4 0.0 all-reduce.5.cloned.1.call-start
  89.5 130.9 %all-reduce.3.cloned.1.call-done = f32[512,512]{1,0:T(8,128)} async-done(((f32[512,512]{1,0:T(8,128)}), f32[512,512]{1,0:T(8,128)}) %all-reduce.3.cloned.1.call-update) | async-done | bytes 1048592 | tf_op jit(solution)/shard_map/psum | solution.py:20
  220.4 4.0 %fusion.9 = f32[512,512]{1,0:T(8,128)S(1)} fusion(f32[512,512]{1,0:T(8,128)} %all-reduce.3.cloned.1.call-done), kind=kOutput, calls=%fused_computation.15 | convolution fusion | flops 1611399168 | bytes 2097152 | tf_op jit(solution)/shard_map/dot_general | solution.py:47
  224.4 8.1 %multiply_add_fusion = f32[512,1024]{0,1:T(8,128)S(1)} fusion(f32[512,512]{1,0:T(8,128)S(1)} %fusion.9, f32[]{:T(128)S(6)} %div.3, f32[512,1,1024]{0,2,1:T(8,128)} %copy.11, f32[1024,512]{1,0:T(8,128)} %copy-done), kind=kOutput, calls=%fused_computation.5 | convolution fusion | flops 3228565504 | bytes 7340036 | tf_op jit(solution)/shard_map/dot_general | solution.py:50
  232.5 4.5 %fusion.13 = f32[512,512]{1,0:T(8,128)} fusion(f32[512,1024]{0,1:T(8,128)S(1)} %multiply_add_fusion), kind=kOutput, calls=%fused_computation.20 | convolution fusion | flops 3221225472 | bytes 3145728 | tf_op jit(solution)/shard_map/dot_general | solution.py:17
  237.0 0.0 all-reduce.5.cloned.1.call-update
  237.0 6.0 %copy.15 = f32[512,1,1024]{2,1,0:T(1,128)} copy(f32[512,1,1024]{0,2,1:T(8,128)} %get-tuple-element.7) | data formatting | bytes 4194304
  243.1 123.7 %all-reduce.5.cloned.1.call-done = f32[512,512]{1,0:T(8,128)} async-done(((f32[512,512]{1,0:T(8,128)}), f32[512,512]{1,0:T(8,128)}) %all-reduce.5.cloned.1.call-update) | async-done | bytes 1048592 | tf_op jit(solution)/shard_map/psum | solution.py:20
  366.8 4.0 %fusion.8 = f32[512,512]{1,0:T(8,128)S(1)} fusion(f32[512,512]{1,0:T(8,128)} %all-reduce.5.cloned.1.call-done), kind=kOutput, calls=%fused_computation.13 | convolution fusion | flops 1611399168 | bytes 2097152 | tf_op jit(solution)/shard_map/dot_general | solution.py:47
  370.8 4.9 %multiply_bitcast_fusion = f32[512,1,1024]{0,2,1:T(8,128)} fusion(f32[512,1024]{0,1:T(8,128)S(1)} %multiply_add_fusion, f32[512,512]{1,0:T(8,128)S(1)} %fusion.8), kind=kOutput, calls=%fused_computation.4 | convolution fusion | flops 3222798336 | bytes 5242880 | tf_op jit(solution)/shard_map/dot_general | solution.py:50
  375.8 6.0 %copy.16 = f32[512,1,1024]{2,1,0:T(1,128)} copy(f32[512,1,1024]{0,2,1:T(8,128)} %multiply_bitcast_fusion) | data formatting | bytes 4194304
  (7 shorter events, 0.0 us)
Async XLA Ops:
  10.4 6.2 %copy-start.2 = (f32[512,1,1024]{2,1,0:T(1,128)S(1)}, f32[512,1,1024]{2,1,0:T(1,128)}, u32[]{:S(2)}) copy-start(f32[512,1,1024]{2,1,0:T(1,128)} %param.7) | copy-start | bytes 6291460
  11.5 25.5 %all-to-all-start = ((bf16[128,4,1024]{2,0,1:T(8,128)(2,1)}), bf16[128,4,1024]{2,0,1:T(8,128)(2,1)S(1)}, u32[]{:S(2)}, u32[]{:S(2)}) async-start(bf16[128,4,1024]{2,0,1:T(8,128)(2,1)} %bitcast.58), calls=%async_computation | async-start | bytes 2097152 | tf_op jit(solution)/shard_map/all_to_all | solution.py:31
  16.7 4.4 %copy-start.3 = (bf16[128,512]{1,0:T(8,128)(2,1)S(1)}, bf16[128,512]{1,0:T(8,128)(2,1)}, u32[]{:S(2)}) copy-start(bf16[128,512]{1,0:T(8,128)(2,1)} %param.4) | copy-start | bytes 393220
  16.7 203.7 %all-reduce.3.cloned.1.call-start = ((), (), s32[]{:S(2)}) async-start(), calls=%async_computation.1 | async-start | bytes 2097152 | tf_op jit(solution)/shard_map/psum | solution.py:20
  37.0 1.9 copy-start.1
  38.9 43.0 %copy-start = (f32[1024,512]{1,0:T(8,128)}, f32[1024,512]{1,0:T(8,128)S(1)}, u32[]{:S(2)}) copy-start(f32[1024,512]{1,0:T(8,128)S(1)} %fusion.12) | copy-start | bytes 6291460
  89.4 277.4 %all-reduce.5.cloned.1.call-start = ((), (), s32[]{:S(2)}) async-start(), calls=%async_computation.2 | async-start | bytes 2097152 | tf_op jit(solution)/shard_map/psum | solution.py:20
Sparse Core Ops, SparseCore 0:
  89.6 130.7 all-reduce.2
  237.1 129.6 all-reduce.4
where the time goes:
time: 389 us
  waiting for transfers between devices  255 us (66%)
  blocking collectives  55.6 us (14%)
  matrix products  38.2 us (10%)
  local copies, waits for them, and re-layouts  17.5 us (4%)
  between operations  14.7 us (4%)
  starting transfers between devices  5.24 us (1%)
    psum x2, waiting for transfers between devices, gram_total(): return lax.psum(local_gram, ('dp', 'head'))  255 us
    psum x1, blocking collectives, local(): squares = lax.psum(jnp.sum(nesterov * nesterov), ('dp', 'head'))  39.8 us
    unnamed x11, local copies, waits for them, and re-layouts  16.5 us
    all_gather x1, blocking collectives, local(): gathered = lax.all_gather(latents, 'dp', axis=0, tiled=True)  15.9 us
    dot_general x2, matrix products, local(): jnp.dot(polynomial, iterate, precision=lax.Precision.HIGHEST)  13 us
    dot_general x2, matrix products, gram_total(): lax.dot_general(iterate, iterate, (((1,), (1,)), ((), ())), precision=lax...  11.9 us
    dot_general x2, matrix products, local(): jnp.dot(gram_matrix, gram_matrix, precision=lax.Precision.HIGHEST)  8.05 us
  transfers between devices with their start and end apart: 3, of which 2 were waited for; matrix products, arithmetic and copies ran while one was open for 3% of the time, Pallas kernels for 0%

commit v1 on v0

--- a/solution.py
+++ b/solution.py
@@ -17,7 +17,7 @@
     local_gram = lax.dot_general(
         iterate, iterate, (((1,), (1,)), ((), ())), precision=lax.Precision.HIGHEST
     )
-    return lax.psum(local_gram, ("dp", "head"))
+    return jnp.sum(lax.all_gather(local_gram, ("dp", "head")), axis=0)
 
 
 def local(latents, targets, kv_weight, momentum):

time: 389 us -> 535 us (1.38)
  waiting for transfers between devices: 255 us -> 381 us
  other arithmetic: 2.63 us -> 27.4 us
  matrix products: 38.2 us -> 32.2 us
    all_gather x0 -> x2, waiting for transfers between devices: none -> 381 us  [gram_total(): return jnp.sum(lax.all_gather(local_gram, ('dp', 'head')), axis=0)]
    psum x2 -> x0, waiting for transfers between devices: 255 us -> none  [gram_total(): return lax.psum(local_gram, ('dp', 'head'))]
    reduce_sum x0 -> x2, other arithmetic: none -> 24.8 us  [gram_total(): return jnp.sum(lax.all_gather(local_gram, ('dp', 'head')), axis=0)]
    unnamed x11 -> x13, local copies, waits for them, and re-layouts: 16.5 us -> 16.5 us
  transfers between devices with their start and end apart: 3 -> 3, of which waited for: 2 -> 2; matrix products, arithmetic and copies ran while one was open for 3% -> 2% of each run, Pallas kernels for 0% -> 0%
where the time goes in v1:
time: 535 us; the launch traced here: 534 us
  waiting for transfers between devices  381 us (71%)
  blocking collectives  55.6 us (10%)
  matrix products  32.2 us (6%)
  other arithmetic  27.4 us (5%)
  local copies, waits for them, and re-layouts  17.5 us (3%)
  between operations  14.8 us (3%)
  starting transfers between devices  5.42 us (1%)
    all_gather x2, waiting for transfers between devices, gram_total(): return jnp.sum(lax.all_gather(local_gram, ('dp', 'head')), axis=0)  381 us
    psum x1, blocking collectives, local(): squares = lax.psum(jnp.sum(nesterov * nesterov), ('dp', 'head'))  39.7 us
    reduce_sum x2, other arithmetic, gram_total(): return jnp.sum(lax.all_gather(local_gram, ('dp', 'head')), axis=0)  24.8 us
    unnamed x13, local copies, waits for them, and re-layouts  16.5 us
    all_gather x1, blocking collectives, local(): gathered = lax.all_gather(latents, 'dp', axis=0, tiled=True)  15.9 us
    dot_general x2, matrix products, gram_total(): lax.dot_general(iterate, iterate, (((1,), (1,)), ((), ())), precision=lax...  11.9 us
    dot_general x2, matrix products, local(): jnp.dot(polynomial, iterate, precision=lax.Precision.HIGHEST)  11.3 us
  transfers between devices with their start and end apart: 3, of which 2 were waited for; matrix products, arithmetic and copies ran while one was open for 2% of the time, Pallas kernels for 0%

profile of v1, /device:TPU:0, one launch (start us, length us, event | category | flops | bytes accessed | tf_op | source)
XLA Modules:
  0.0 533.8 jit_solution(2059428106916003486)
XLA Ops:
  7.2 3.2 fusion
  10.4 0.0 copy-start.3
  10.4 1.0 copy.21
  11.5 5.2 all-to-all-start
  16.7 4.4 copy.11
  21.1 15.9 %all_gather.15 = bf16[512,512]{1,0:T(8,128)(2,1)} all-gather(bf16[128,512]{1,0:T(8,128)(2,1)S(1)} %copy-done.4), channel_id=1, replica_groups=mesh['dp'=4,'head'=8] {'dp'}, dimensions={0}, use_global_device_ids=true | all-gather | bytes 655360 | tf_op jit(solution)/shard_map/all_gather | solution.py:32
  37.0 1.9 fusion.12
  38.9 2.6 multiply_reduce_fusion
  41.6 39.7 %psum.7 = f32[]{:T(128)} all-reduce(f32[]{:T(128)} %get-tuple-element.6), channel_id=1, replica_groups=mesh['dp'=4,'head'=8] {'dp','head'}, use_global_device_ids=true, to_apply=%region_1.0 | all-reduce | flops 1 | bytes 8 | tf_op jit(solution)/shard_map/psum | solution.py:40
  82.0 7.5 %fusion.3 = f32[512,512]{1,0:T(8,128)} fusion(f32[]{:T(128)S(6)} %div.3, f32[1024,512]{1,0:T(8,128)S(1)} %fusion.12, f32[512,1,1024]{0,2,1:T(8,128)} %copy.11), kind=kOutput, calls=%fused_computation.9 | convolution fusion | flops 3224371200 | bytes 5242884 | tf_op jit(solution)/shard_map/dot_general | solution.py:17
  89.5 0.0 all-gather.5.cloned.1.call-update
  89.5 0.2 all-gather.7.cloned.1.call-start
  89.7 194.3 %all-gather.5.cloned.1.call-done = f32[16384,512]{1,0:T(8,128)} async-done(((f32[512,512]{1,0:T(8,128)}), f32[16384,512]{1,0:T(8,128)}) %all-gather.5.cloned.1.call-update) | async-done | bytes 33554448 | tf_op jit(solution)/shard_map/all_gather | solution.py:20
  284.1 12.3 %reduce_sum.28 = f32[512,512]{1,0:T(8,128)S(1)} reduce(f32[32,512,512]{2,1,0:T(8,128)} %bitcast.62, f32[]{:T(128)} %constant.3.clone.1), dimensions={0}, to_apply=%region_2.0 | reduce | flops 8126464 | bytes 34603012 | tf_op jit(solution)/shard_map/reduce_sum | solution.py:20
  296.4 1.9 fusion.9
  298.3 6.3 %multiply_add_fusion = f32[512,1024]{0,1:T(8,128)S(1)} fusion(f32[512,512]{1,0:T(8,128)S(1)} %fusion.9, f32[]{:T(128)S(6)} %div.3, f32[512,1,1024]{0,2,1:T(8,128)} %copy.11, f32[1024,512]{1,0:T(8,128)S(1)} %copy-done.1), kind=kOutput, calls=%fused_computation.5 | convolution fusion | flops 3228565504 | bytes 7340036 | tf_op jit(solution)/shard_map/dot_general | solution.py:50
  304.6 4.5 fusion.13
  309.1 0.0 all-gather.7.cloned.1.call-update
  309.2 6.0 %copy.15 = f32[512,1,1024]{2,1,0:T(1,128)} copy(f32[512,1,1024]{0,2,1:T(8,128)} %get-tuple-element.7) | data formatting | bytes 4194304
  315.2 186.5 %all-gather.7.cloned.1.call-done = f32[16384,512]{1,0:T(8,128)} async-done(((f32[512,512]{1,0:T(8,128)}), f32[16384,512]{1,0:T(8,128)}) %all-gather.7.cloned.1.call-update) | async-done | bytes 33554448 | tf_op jit(solution)/shard_map/all_gather | solution.py:20
  501.7 12.5 %reduce_sum.29 = f32[512,512]{1,0:T(8,128)S(1)} reduce(f32[32,512,512]{2,1,0:T(8,128)} %bitcast.61, f32[]{:T(128)} %constant.3.clone.1), dimensions={0}, to_apply=%region_3.0 | reduce | flops 8126464 | bytes 34603012 | tf_op jit(solution)/shard_map/reduce_sum | solution.py:20
  514.2 1.9 fusion.8
  516.1 4.9 multiply_bitcast_fusion
  521.0 6.0 %copy.16 = f32[512,1,1024]{2,1,0:T(1,128)} copy(f32[512,1,1024]{0,2,1:T(8,128)} %multiply_bitcast_fusion) | data formatting | bytes 4194304
  (11 shorter events, 0.0 us)
Async XLA Ops:
  10.4 6.2 %copy-start.3 = (f32[512,1,1024]{2,1,0:T(1,128)S(1)}, f32[512,1,1024]{2,1,0:T(1,128)}, u32[]{:S(2)}) copy-start(f32[512,1,1024]{2,1,0:T(1,128)} %param.7) | copy-start | bytes 6291460
  11.5 25.5 %all-to-all-start = ((bf16[128,4,1024]{2,0,1:T(8,128)(2,1)}), bf16[128,4,1024]{2,0,1:T(8,128)(2,1)S(1)}, u32[]{:S(2)}, u32[]{:S(2)}) async-start(bf16[128,4,1024]{2,0,1:T(8,128)(2,1)} %bitcast.60), calls=%async_computation | async-start | bytes 2097152 | tf_op jit(solution)/shard_map/all_to_all | solution.py:31
  16.7 4.4 copy-start.4
  16.7 267.4 %all-gather.5.cloned.1.call-start = ((), (), s32[]{:S(2)}) async-start(), calls=%async_computation.1 | async-start | bytes 34603008 | tf_op jit(solution)/shard_map/all_gather | solution.py:20
  37.0 1.9 copy-start.2
  38.9 43.1 %copy-start = (f32[1024,512]{1,0:T(8,128)}, f32[1024,512]{1,0:T(8,128)S(1)}, u32[]{:S(2)}) copy-start(f32[1024,512]{1,0:T(8,128)S(1)} %fusion.12) | copy-start | bytes 6291460
  89.5 412.2 %all-gather.7.cloned.1.call-start = ((), (), s32[]{:S(2)}) async-start(), calls=%async_computation.2 | async-start | bytes 34603008 | tf_op jit(solution)/shard_map/all_gather | solution.py:20
  296.4 1.9 copy-start.1
Sparse Core Ops, SparseCore 0:
  89.6 194.4 all-gather.4
  309.3 192.3 all-gather.6
